TPU v7x, 32 devices: a whole 2x2x4 slice. The times are simulated.
32 devices in a mesh: bucket: 16 (over z, y, core), edge: 2 (over x).
Axes of the slice: x: 2, y: 2, z: 4, core: 2. Of those that a mesh axis runs over, the one named last changes fastest.
Arguments:
- left_slab: bfloat16 [6144, 256], P(('bucket', 'edge')), may hold values from -1.5 to 1.5
- right_slab: bfloat16 [6144, 256], P(('bucket', 'edge')), may hold values from -1.5 to 1.5
- relation: float32 [1024, 256], replicated, may hold values from 0.5 to 1.5
- src_ids: int32 [2, 16, 4096], P(None, 'bucket', 'edge'), may hold values from 0 to 383
- dst_ids: int32 [2, 16, 4096], P(None, 'bucket', 'edge'), may hold values from 0 to 383
- rel_ids: int32 [2, 16, 4096], P(None, 'bucket', 'edge'), may hold values from 0 to 1023
- neg_ids: int32 [2, 16, 16, 512], P(None, 'bucket', 'edge'), may hold values from 0 to 383
- edge_counts: int32 [2, 16], P(None, 'bucket'), may hold values from 1 to 4096, as said below
Outputs:
- left_out: bfloat16 [6144, 256], P(('bucket', 'edge'))
- right_out: bfloat16 [6144, 256], P(('bucket', 'edge'))
- relation_out: float32 [1024, 256], replicated
Inputs may be any that keep to these rules, and one draw needn't show every extreme that they name: `edge_counts`: live edges are the first slots of a bucket; in every round some bucket has all 4096 slots live.
All inputs are finite; a program needn't handle non-finite values.
Results may differ from a plain program's by a relative error of at most 0.0046.
Values may be sent and summed in bfloat16 or wider, within the bound.
A program may use at most 64 MiB of HBM per device.

v0:
```python
import jax
import jax.numpy as jnp
from jax import lax
from jax.sharding import PartitionSpec as P

ROUNDS = 2
learn_rate = 0.05
relation_rate = 0.05


def from_behind(block, axis, distance):
    devices = range(lax.axis_size(axis))
    route = [((i - distance) % len(devices), i) for i in devices]
    return lax.ppermute(block, axis, route)


def span_grads(left, right, theta, src_c, dst_c, rel_c, neg_c, mask):
    s_rows = left[src_c]
    d_rows = right[dst_c]
    negatives = right[neg_c]
    t_rows = theta[rel_c]
    s_wide = s_rows.astype(jnp.float32)
    q_rows = (s_wide * t_rows).astype(jnp.bfloat16)
    q_wide = q_rows.astype(jnp.float32)
    d_wide = d_rows.astype(jnp.float32)
    pos = jnp.sum(q_wide * d_wide, axis=-1)
    scores = jnp.dot(q_rows, negatives.T, preferred_element_type=jnp.float32)
    g_pos = -jax.nn.sigmoid(-pos) * mask
    g_neg = (jax.nn.sigmoid(scores) * mask[:, None]).astype(jnp.bfloat16)
    g_q = g_pos[:, None] * d_wide + jnp.dot(g_neg, negatives, preferred_element_type=jnp.float32)
    g_d = g_pos[:, None] * q_wide
    g_negrows = jnp.dot(g_neg.T, q_rows, preferred_element_type=jnp.float32)
    g_s = g_q * t_rows
    g_t = g_q * s_wide
    return (g_s, g_d, g_negrows, g_t)


def train(full_left, full_right, theta, src, dst, rel, neg, block_ids, count):
    width = src.shape[1]
    n_live = jnp.sum((block_ids * width < count).astype(jnp.int32))

    def step(c, carry):
        g_left, g_right, g_theta = carry
        src_c = lax.dynamic_index_in_dim(src, c, 0, keepdims=False)
        dst_c = lax.dynamic_index_in_dim(dst, c, 0, keepdims=False)
        rel_c = lax.dynamic_index_in_dim(rel, c, 0, keepdims=False)
        neg_c = lax.dynamic_index_in_dim(neg, c, 0, keepdims=False)
        first = lax.dynamic_index_in_dim(block_ids, c, 0, keepdims=False) * width
        mask = (first + jnp.arange(width) < count).astype(jnp.float32)
        g_s, g_d, g_negrows, g_t = span_grads(
            full_left, full_right, theta, src_c, dst_c, rel_c, neg_c, mask
        )
        g_left = g_left.at[src_c].add(g_s)
        g_right = g_right.at[dst_c].add(g_d).at[neg_c].add(g_negrows)
        g_theta = g_theta.at[rel_c].add(g_t)
        return (g_left, g_right, g_theta)

    rows = full_left.shape[0]
    init = (
        jnp.zeros((rows, full_left.shape[1]), jnp.float32),
        jnp.zeros((rows, full_left.shape[1]), jnp.float32),
        jnp.zeros(theta.shape, jnp.float32),
    )
    return lax.fori_loop(0, n_live, step, init)


def relation_sum(g_theta):
    return lax.psum(g_theta, ("bucket", "edge"))


def descend(slab, grad):
    return (slab.astype(jnp.float32) - learn_rate * grad).astype(jnp.bfloat16)


def body(left_slab, right_slab, relation, src_ids, dst_ids, rel_ids, neg_ids, edge_counts):
    me = lax.axis_index("edge")
    blocks = neg_ids.shape[2]
    width = src_ids.shape[2] // blocks
    negs = neg_ids.shape[3]
    src = src_ids.reshape(ROUNDS, blocks, width)
    dst = dst_ids.reshape(ROUNDS, blocks, width)
    rel = rel_ids.reshape(ROUNDS, blocks, width)
    neg = neg_ids.reshape(ROUNDS, blocks, negs)
    positions = jnp.arange(blocks, dtype=jnp.int32)
    block_ids = me * blocks + positions
    theta = relation
    left_out = left_slab
    right_out = right_slab
    for rnd in range(ROUNDS):
        if rnd > 0:
            right_out = from_behind(right_out, "bucket", 1)
        full_left, full_right = (
            lax.all_gather(left_out, "edge", axis=0, tiled=True),
            lax.all_gather(right_out, "edge", axis=0, tiled=True),
        )
        g_left, g_right, g_theta = train(
            full_left,
            full_right,
            theta,
            src[rnd],
            dst[rnd],
            rel[rnd],
            neg[rnd],
            block_ids,
            edge_counts[rnd, 0],
        )
        g_left, g_right = (
            lax.psum_scatter(g_left, "edge", scatter_dimension=0, tiled=True),
            lax.psum_scatter(g_right, "edge", scatter_dimension=0, tiled=True),
        )
        left_out = descend(left_out, g_left)
        right_out = descend(right_out, g_right)
        theta = theta - relation_rate * relation_sum(g_theta)
    return (left_out, right_out, theta)


def solution(mesh):
    placed = (
        P(("bucket", "edge"), None),
        P(("bucket", "edge"), None),
        P(),
        P(None, "bucket", "edge"),
        P(None, "bucket", "edge"),
        P(None, "bucket", "edge"),
        P(None, "bucket", "edge", None),
        P(None, "bucket"),
    )
    return jax.shard_map(
        body,
        mesh=mesh,
        in_specs=placed,
        out_specs=(P(("bucket", "edge"), None), P(("bucket", "edge"), None), P()),
        check_vma=False,
    )
```

profile of v0, /device:TPU:0, one launch (start us, length us, event | category | flops | bytes accessed | tf_op | source)
XLA Modules:
  0.0 697.3 jit_solution(16866233475655808648)
XLA Ops:
  12.7 6.5 all_gather.12
  19.3 5.4 all_gather.13
  27.8 73.1 %while.28 = (s32[]{:T(128)}, f32[384,256]{1,0:T(8,128)}, f32[384,256]{1,0:T(8,128)S(1)}, f32[1024,256]{1,0:T(8,128)}, s32[]{:T(128)}, /*index=5*/s32[8,256]{1,0:...) while((s32[]{:T(128)}, f32[384,256]{1,0:T(8,128)}, ...), condition=%wide.region_7.8_spmd, body=%wide.region_1.7_spmd.sunk | while | flops 203302656 | bytes 9221379 | solution.py:64
  34.2 2.0 gather_fusion.3
  38.4 3.6 scatter_custom_fusion.31
  42.3 2.2 scatter_custom_fusion.32
  44.5 3.5 scatter_fusion
  48.0 4.0 scatter_custom_fusion.34
  58.4 2.0 gather_fusion.3
  62.6 3.6 scatter_custom_fusion.31
  66.4 2.2 scatter_custom_fusion.32
  68.6 3.5 scatter_fusion
  72.1 4.0 scatter_custom_fusion.34
  82.5 2.0 gather_fusion.3
  86.7 3.6 scatter_custom_fusion.31
  90.5 2.2 scatter_custom_fusion.32
  92.8 3.5 scatter_fusion
  96.3 4.0 scatter_custom_fusion.34
  104.3 250.2 %all-reduce.3.cloned.1.call-done = f32[1024,256]{1,0:T(8,128)} async-done(((f32[1024,256]{1,0:T(8,128)}), f32[1024,256]{1,0:T(8,128)}) %all-reduce.3.cloned.1.call-update) | async-done | bytes 1048592 | tf_op jit(solution)/shard_map/psum | solution.py:68
  357.9 5.8 all_gather.14
  363.8 5.7 all_gather.15
  371.3 183.4 %while.29 = (s32[]{:T(128)}, f32[384,256]{1,0:T(8,128)}, f32[384,256]{1,0:T(8,128)S(1)}, f32[1024,256]{1,0:T(8,128)}, s32[]{:T(128)}, /*index=5*/s32[8,256]{1,0:...) while((s32[]{:T(128)}, f32[384,256]{1,0:T(8,128)}, ...), condition=%wide.region_18.19_spmd, body=%wide.region_12.18_spmd.sunk | while | flops 203302656 | bytes 9221379 | solution.py:64
  376.4 2.0 gather_fusion.7
  380.8 3.6 scatter_custom_fusion.38
  384.6 2.2 scatter_custom_fusion.39
  386.8 3.5 scatter_fusion.1
  390.3 4.0 scatter_custom_fusion.41
  399.3 2.0 gather_fusion.7
  403.6 3.6 scatter_custom_fusion.38
  407.4 2.2 scatter_custom_fusion.39
  409.7 3.5 scatter_fusion.1
  413.2 4.0 scatter_custom_fusion.41
  422.1 2.0 gather_fusion.7
  426.4 3.6 scatter_custom_fusion.38
  430.2 2.2 scatter_custom_fusion.39
  432.5 3.5 scatter_fusion.1
  436.0 4.0 scatter_custom_fusion.41
  444.9 2.0 gather_fusion.7
  449.2 3.6 scatter_custom_fusion.38
  453.1 2.2 scatter_custom_fusion.39
  455.3 3.5 scatter_fusion.1
  458.8 4.0 scatter_custom_fusion.41
  467.7 2.0 gather_fusion.7
  472.1 3.6 scatter_custom_fusion.38
  475.9 2.2 scatter_custom_fusion.39
  478.1 3.5 scatter_fusion.1
  481.6 4.0 scatter_custom_fusion.41
  490.5 2.0 gather_fusion.7
  494.9 3.6 scatter_custom_fusion.38
  498.7 2.2 scatter_custom_fusion.39
  500.9 3.5 scatter_fusion.1
  504.4 4.0 scatter_custom_fusion.41
  513.4 2.0 gather_fusion.7
  517.7 3.6 scatter_custom_fusion.38
  521.5 2.2 scatter_custom_fusion.39
  523.8 3.5 scatter_fusion.1
  527.3 4.0 scatter_custom_fusion.41
  536.2 2.0 gather_fusion.7
  540.5 3.6 scatter_custom_fusion.38
  544.4 2.2 scatter_custom_fusion.39
  546.6 3.5 scatter_fusion.1
  550.1 4.0 scatter_custom_fusion.41
  556.8 127.4 %all-reduce.5.cloned.1.call-done = f32[1024,256]{1,0:T(8,128)} async-done(((f32[1024,256]{1,0:T(8,128)}), f32[1024,256]{1,0:T(8,128)}) %all-reduce.5.cloned.1.call-update) | async-done | bytes 1048592 | tf_op jit(solution)/shard_map/psum | solution.py:68
  684.2 2.3 multiply_subtract_fusion
  (248 shorter events, 94.2 us)
Async XLA Ops:
  8.0 346.5 %all-reduce.3.cloned.1.call-start = ((), (), s32[]{:S(2)}) async-start(), calls=%async_computation.5 | async-start | bytes 2097152 | tf_op jit(solution)/shard_map/psum | solution.py:68
  8.0 0.7 copy-start.9
  9.4 1.4 copy-start.8
  9.4 3.4 copy-start.7
  10.1 2.6 copy-start.4
  12.7 6.6 copy-start.3
  19.3 8.6 %copy-start.2 = (f32[1024,256]{1,0:T(8,128)S(1)}, f32[1024,256]{1,0:T(8,128)}, u32[]{:S(2)}) copy-start(f32[1024,256]{1,0:T(8,128)} %param.14) | copy-start | bytes 3145732
  101.0 0.7 copy-start.1
  101.7 254.2 %reduce-scatter.7.cloned.1.call-start = ((), (), s32[]{:S(2)}) async-start(), calls=%async_computation.6 | async-start | bytes 589824 | tf_op jit(solution)/shard_map/reduce_scatter | solution.py:109
  102.3 254.7 %reduce-scatter.5.cloned.1.call-start = ((), (), s32[]{:S(2)}) async-start(), calls=%async_computation.4 | async-start | bytes 589824 | tf_op jit(solution)/shard_map/reduce_scatter | solution.py:108
  102.9 581.3 %all-reduce.5.cloned.1.call-start = ((), (), s32[]{:S(2)}) async-start(), calls=%async_computation.9 | async-start | bytes 2097152 | tf_op jit(solution)/shard_map/psum | solution.py:68
  356.9 6.9 collective-permute-start
  363.8 5.7 copy-start.5
  554.7 0.7 copy-start
  555.5 131.1 %reduce-scatter.9.cloned.1.call-start = ((), (), s32[]{:S(2)}) async-start(), calls=%async_computation.7 | async-start | bytes 589824 | tf_op jit(solution)/shard_map/reduce_scatter | solution.py:108
  556.0 132.1 %reduce-scatter.11.cloned.1.call-start = ((), (), s32[]{:S(2)}) async-start(), calls=%async_computation.8 | async-start | bytes 589824 | tf_op jit(solution)/shard_map/reduce_scatter | solution.py:109
  686.5 1.6 copy-start.6
Sparse Core Ops, SparseCore 0:
  101.1 253.3 all-reduce.2
  554.9 129.2 all-reduce.4
Sparse Core Ops, SparseCore 1:
  104.4 134.6 reduce-scatter.6
  241.2 13.3 reduce-scatter.4
  558.2 10.5 reduce-scatter.8
  571.0 13.3 reduce-scatter.10
where the time goes:
time: 700 us; the launch traced here: 697 us
  waiting for transfers between devices  380 us (54%)
  other arithmetic  178 us (25%)
  local copies, waits for them, and re-layouts  74 us (11%)
  blocking collectives  23.5 us (3%)
  loops' own time  16.6 us (2%)
  between operations  15.8 us (2%)
  matrix products  9.18 us (1%)
    psum x2, waiting for transfers between devices, relation_sum(): return lax.psum(g_theta, ('bucket', 'edge'))  378 us
    scatter-add x22, other arithmetic, step(): g_right = g_right.at[dst_c].add(g_d).at[neg_c].add(g_negrows)  62.9 us
    scatter-add x11, other arithmetic, step(): g_theta = g_theta.at[rel_c].add(g_t)  43.8 us
    scatter-add x11, other arithmetic, step(): g_left = g_left.at[src_c].add(g_s)  39.1 us
    gather x11, local copies, waits for them, and re-layouts, span_grads(): negatives = right[neg_c]  21.5 us
    another operation x2, loops' own time, train(): return lax.fori_loop(0, n_live, step, init)  16.6 us
  transfers between devices with their start and end apart: 7, of which 2 were waited for; matrix products, arithmetic and copies ran while one was open for 1% of the time, Pallas kernels for 0%

commit v1 on v0

--- a/solution.py
+++ b/solution.py
@@ -65,7 +65,7 @@
 
 
 def relation_sum(g_theta):
-    return lax.psum(g_theta, ("bucket", "edge"))
+    return jnp.sum(lax.all_gather(g_theta, ("bucket", "edge")), axis=0)
 
 
 def descend(slab, grad):

time: 700 us -> 827 us (1.18)
  waiting for transfers between devices: 380 us -> 491 us
  other arithmetic: 178 us -> 192 us
    psum x2 -> x0, waiting for transfers between devices: 378 us -> none  [relation_sum(): return lax.psum(g_theta, ('bucket', 'edge'))]
    all_gather x0 -> x2, waiting for transfers between devices: none -> 327 us  [relation_sum(): return jnp.sum(lax.all_gather(g_theta, ('bucket', 'edge')), axis=0)]
    reduce_scatter x2, waiting for transfers between devices: 0.03 us -> 139 us  [body(): lax.psum_scatter(g_right, 'edge', scatter_dimension=0, tiled=True)]
    reduce_sum x0 -> x2, other arithmetic: none -> 24.8 us  [relation_sum(): return jnp.sum(lax.all_gather(g_theta, ('bucket', 'edge')), axis=0)]
    reduce_scatter x2, waiting for transfers between devices: 0.03 us -> 24.1 us  [body(): lax.psum_scatter(g_left, 'edge', scatter_dimension=0, tiled=True)]
  transfers between devices with their start and end apart: 7 -> 7, of which waited for: 2 -> 6; matrix products, arithmetic and copies ran while one was open for 1% -> 1% of each run, Pallas kernels for 0% -> 0%
where the time goes in v1:
time: 827 us; the launch traced here: 824 us
  waiting for transfers between devices  491 us (59%)
  other arithmetic  192 us (23%)
  local copies, waits for them, and re-layouts  76.2 us (9%)
  blocking collectives  22.7 us (3%)
  loops' own time  17.4 us (2%)
  between operations  15.4 us (2%)
  matrix products  9.15 us (1%)
    all_gather x2, waiting for transfers between devices, relation_sum(): return jnp.sum(lax.all_gather(g_theta, ('bucket', 'edge')), axis=0)  327 us
    reduce_scatter x2, waiting for transfers between devices, body(): lax.psum_scatter(g_right, 'edge', scatter_dimension=0, tiled=True)  139 us
    scatter-add x22, other arithmetic, step(): g_right = g_right.at[dst_c].add(g_d).at[neg_c].add(g_negrows)  62.9 us
    scatter-add x11, other arithmetic, step(): g_theta = g_theta.at[rel_c].add(g_t)  43.8 us
    scatter-add x11, other arithmetic, step(): g_left = g_left.at[src_c].add(g_s)  34.7 us
    reduce_sum x2, other arithmetic, relation_sum(): return jnp.sum(lax.all_gather(g_theta, ('bucket', 'edge')), axis=0)  24.8 us
    reduce_scatter x2, waiting for transfers between devices, body(): lax.psum_scatter(g_left, 'edge', scatter_dimension=0, tiled=True)  24.1 us
    gather x11, local copies, waits for them, and re-layouts, span_grads(): negatives = right[neg_c]  21.5 us
  transfers between devices with their start and end apart: 7, of which 6 were waited for; matrix products, arithmetic and copies ran while one was open for 1% of the time, Pallas kernels for 0%

profile of v1, /device:TPU:0, one launch (start us, length us, event | category | flops | bytes accessed | tf_op | source)
XLA Modules:
  0.0 824.5 jit_solution(8552959032936717649)
XLA Ops:
  11.7 6.7 all_gather.24
  18.4 5.5 all_gather.25
  26.3 68.6 %while.28 = (s32[]{:T(128)}, f32[384,256]{1,0:T(8,128)S(1)}, f32[384,256]{1,0:T(8,128)S(1)}, f32[1024,256]{1,0:T(8,128)}, s32[]{:T(128)}, /*index=5*/s32[8,256]{...) while((s32[]{:T(128)}, f32[384,256]{1,0:T(8,128)S(1)}, ...), condition=%wide.region_7.8_spmd, body=%wide.region_1.7_spmd.sunk | while | flops 203302656 | bytes 9221379 | solution.py:64
  31.3 2.0 gather_fusion.3
  33.3 2.2 gather_fusion.1
  36.8 2.2 scatter_custom_fusion.31
  39.3 2.2 scatter_custom_fusion.32
  41.5 3.5 scatter_fusion
  45.0 4.0 scatter_custom_fusion.34
  53.9 2.0 gather_fusion.3
  55.9 2.2 gather_fusion.1
  59.5 2.2 scatter_custom_fusion.31
  61.9 2.2 scatter_custom_fusion.32
  64.1 3.5 scatter_fusion
  67.6 4.0 scatter_custom_fusion.34
  76.5 2.0 gather_fusion.3
  78.5 2.2 gather_fusion.1
  82.1 2.2 scatter_custom_fusion.31
  84.5 2.2 scatter_custom_fusion.32
  86.7 3.5 scatter_fusion
  90.2 4.0 scatter_custom_fusion.34
  98.3 124.3 %reduce-scatter.7.cloned.1.call-done = f32[192,256]{1,0:T(8,128)} async-done(((f32[384,256]{1,0:T(8,128)}), f32[192,256]{1,0:T(8,128)}) %reduce-scatter.7.cloned.1.call-update) | async-done | bytes 196624 | tf_op jit(solution)/shard_map/reduce_scatter | solution.py:109
  223.7 14.9 %reduce-scatter.5.cloned.1.call-done = f32[192,256]{1,0:T(8,128)} async-done(((f32[384,256]{1,0:T(8,128)}), f32[192,256]{1,0:T(8,128)}) %reduce-scatter.5.cloned.1.call-update) | async-done | bytes 196624 | tf_op jit(solution)/shard_map/reduce_scatter | solution.py:108
  239.6 5.3 all_gather.26
  244.9 5.3 all_gather.29
  250.1 159.1 %all-gather.5.cloned.1.call-done = f32[32768,256]{1,0:T(8,128)} async-done(((f32[1024,256]{1,0:T(8,128)}), f32[32768,256]{1,0:T(8,128)}) %all-gather.5.cloned.1.call-update) | async-done | bytes 33554448 | tf_op jit(solution)/shard_map/all_gather | solution.py:68
  409.2 12.9 %reduce_sum.56 = f32[1024,256]{1,0:T(8,128)} reduce(f32[32,1024,256]{2,1,0:T(8,128)} %bitcast.102, f32[]{:T(128)} %constant.78.clone.1), dimensions={0}, to_apply=%region_11.12 | reduce | flops 8126464 | bytes 34603012 | tf_op jit(solution)/shard_map/reduce_sum | solution.py:68
  425.3 182.9 %while.29 = (s32[]{:T(128)}, f32[384,256]{1,0:T(8,128)}, f32[384,256]{1,0:T(8,128)S(1)}, f32[1024,256]{1,0:T(8,128)}, s32[]{:T(128)}, /*index=5*/s32[8,256]{1,0:...) while((s32[]{:T(128)}, f32[384,256]{1,0:T(8,128)}, ...), condition=%wide.region_18.19_spmd, body=%wide.region_12.18_spmd.sunk | while | flops 203302656 | bytes 9221379 | solution.py:64
  434.7 3.5 scatter_custom_fusion.38
  438.5 2.2 scatter_custom_fusion.39
  440.8 3.5 scatter_fusion.1
  444.3 4.0 scatter_custom_fusion.41
  457.5 3.5 scatter_custom_fusion.38
  461.3 2.2 scatter_custom_fusion.39
  463.5 3.5 scatter_fusion.1
  467.0 4.0 scatter_custom_fusion.41
  480.3 3.5 scatter_custom_fusion.38
  484.1 2.2 scatter_custom_fusion.39
  486.3 3.5 scatter_fusion.1
  489.8 4.0 scatter_custom_fusion.41
  503.0 3.5 scatter_custom_fusion.38
  506.8 2.2 scatter_custom_fusion.39
  509.1 3.5 scatter_fusion.1
  512.6 4.0 scatter_custom_fusion.41
  525.8 3.5 scatter_custom_fusion.38
  529.6 2.2 scatter_custom_fusion.39
  531.8 3.5 scatter_fusion.1
  535.3 4.0 scatter_custom_fusion.41
  548.5 3.5 scatter_custom_fusion.38
  552.3 2.2 scatter_custom_fusion.39
  554.6 3.5 scatter_fusion.1
  558.1 4.0 scatter_custom_fusion.41
  571.3 3.5 scatter_custom_fusion.38
  575.1 2.2 scatter_custom_fusion.39
  577.3 3.5 scatter_fusion.1
  580.8 4.0 scatter_custom_fusion.41
  594.1 3.5 scatter_custom_fusion.38
  597.9 2.2 scatter_custom_fusion.39
  600.1 3.5 scatter_fusion.1
  603.6 4.0 scatter_custom_fusion.41
  609.6 9.2 %reduce-scatter.9.cloned.1.call-done = f32[192,256]{1,0:T(8,128)} async-done(((f32[384,256]{1,0:T(8,128)}), f32[192,256]{1,0:T(8,128)}) %reduce-scatter.9.cloned.1.call-update) | async-done | bytes 196624 | tf_op jit(solution)/shard_map/reduce_scatter | solution.py:108
  620.4 14.3 %reduce-scatter.11.cloned.1.call-done = f32[192,256]{1,0:T(8,128)} async-done(((f32[384,256]{1,0:T(8,128)}), f32[192,256]{1,0:T(8,128)}) %reduce-scatter.11.cloned.1.call-update) | async-done | bytes 196624 | tf_op jit(solution)/shard_map/reduce_scatter | solution.py:109
  636.4 167.9 %all-gather.7.cloned.1.call-done = f32[32768,256]{1,0:T(8,128)} async-done(((f32[1024,256]{1,0:T(8,128)}), f32[32768,256]{1,0:T(8,128)}) %all-gather.7.cloned.1.call-update) | async-done | bytes 33554448 | tf_op jit(solution)/shard_map/all_gather | solution.py:68
  804.3 11.9 %reduce_sum.57 = f32[1024,256]{1,0:T(8,128)S(1)} reduce(f32[32,1024,256]{2,1,0:T(8,128)} %bitcast.103, f32[]{:T(128)} %constant.78.clone.1), dimensions={0}, to_apply=%region_21.22 | reduce | flops 8126464 | bytes 34603012 | tf_op jit(solution)/shard_map/reduce_sum | solution.py:68
  (244 shorter events, 100.5 us)
Async XLA Ops:
  8.0 214.7 %reduce-scatter.7.cloned.1.call-start = ((), (), s32[]{:S(2)}) async-start(), calls=%async_computation.5 | async-start | bytes 589824 | tf_op jit(solution)/shard_map/reduce_scatter | solution.py:109
  26.3 196.3 %copy-start.4 = (bf16[192,256]{1,0:T(8,128)(2,1)S(1)}, bf16[192,256]{1,0:T(8,128)(2,1)}, u32[]{:S(2)}) copy-start(bf16[192,256]{1,0:T(8,128)(2,1)} %param.13) | copy-start | bytes 294916
  26.3 212.3 %copy-start.5 = (bf16[192,256]{1,0:T(8,128)(2,1)S(1)}, bf16[192,256]{1,0:T(8,128)(2,1)}, u32[]{:S(2)}) copy-start(bf16[192,256]{1,0:T(8,128)(2,1)} %param.12) | copy-start | bytes 294916
  94.9 0.7 copy-start
  94.9 0.9 copy-start.3
  94.9 327.2 %copy-start.2 = (f32[1024,256]{1,0:T(8,128)S(1)}, f32[1024,256]{1,0:T(8,128)}, u32[]{:S(2)}) copy-start(f32[1024,256]{1,0:T(8,128)} %get-tuple-element.544) | copy-start | bytes 3145732
  95.7 142.9 %reduce-scatter.5.cloned.1.call-start = ((), (), s32[]{:S(2)}) async-start(), calls=%async_computation.4 | async-start | bytes 589824 | tf_op jit(solution)/shard_map/reduce_scatter | solution.py:108
  96.4 312.8 %all-gather.5.cloned.1.call-start = ((), (), s32[]{:S(2)}) async-start(), calls=%async_computation.8 | async-start | bytes 34603008 | tf_op jit(solution)/shard_map/all_gather | solution.py:68
  97.0 521.8 %reduce-scatter.9.cloned.1.call-start = ((), (), s32[]{:S(2)}) async-start(), calls=%async_computation.6 | async-start | bytes 589824 | tf_op jit(solution)/shard_map/reduce_scatter | solution.py:108
  223.7 21.2 %collective-permute-start = (bf16[192,256]{1,0:T(8,128)(2,1)S(1)}, bf16[192,256]{1,0:T(8,128)(2,1)S(1)}, u32[]{:S(2)}, u32[]{:S(2)}) collective-permute-start(bf16[192,256]{1,0:T(8,128)(2,1)S(1)} %subtract_convert_fusion.2), channel_id=1, source_target_pairs={{30,0},{0,2},{2,4},{4,6},{6,8},{8,10},{10,12},{12,14},{14,16},{16,... | collective-permute-start | bytes 294920 | tf_op jit(solution)/shard_map/ppermute | solution.py:14
  244.9 180.5 %copy-start.6 = (bf16[192,256]{1,0:T(8,128)(2,1)}, bf16[192,256]{1,0:T(8,128)(2,1)S(1)}, u32[]{:S(2)}) copy-start(bf16[192,256]{1,0:T(8,128)(2,1)S(1)} %collective-permute-done) | copy-start | bytes 294916
  608.2 0.8 copy-start.1
  608.3 26.5 %reduce-scatter.11.cloned.1.call-start = ((), (), s32[]{:S(2)}) async-start(), calls=%async_computation.7 | async-start | bytes 589824 | tf_op jit(solution)/shard_map/reduce_scatter | solution.py:109
  609.0 195.3 %all-gather.7.cloned.1.call-start = ((), (), s32[]{:S(2)}) async-start(), calls=%async_computation.9 | async-start | bytes 34603008 | tf_op jit(solution)/shard_map/all_gather | solution.py:68
Sparse Core Ops, SparseCore 0:
  95.8 126.8 reduce-scatter.6
  224.9 13.6 reduce-scatter.4
  608.4 10.3 reduce-scatter.8
  620.9 13.7 reduce-scatter.10
Sparse Core Ops, SparseCore 1:
  100.6 308.6 all-gather.4
  613.2 191.1 all-gather.6
